TPU v7x, 256 devices: a whole 4x4x8 slice. The times are simulated.
256 devices in a mesh: grp: 32 (over x, y, core), blk: 8 (over z).
Axes of the slice: x: 4, y: 4, z: 8, core: 2. Of those that a mesh axis runs over, the one named last changes fastest.
Arguments:
- tiles_near: bfloat16 [16384, 256, 256], P(('grp', 'blk')), may hold values from -0.078125 to 0.078125
- near_cols: int32 [256, 64], P(('grp', 'blk')), may hold values from 0 to 3
- tiles_far: bfloat16 [6144, 256, 256], P(('grp', 'blk')), may hold values from -0.078125 to 0.078125
- far_groups: int32 [256, 24], P(('grp', 'blk')), may hold values from 0 to 31, as said below
- need_blocks: int32 [256, 32], P(('grp', 'blk')), may hold values from -1 to 3, as said below
- start_vectors: bfloat16 [262144, 128], P(('grp', 'blk')), may hold values from -6 to 6
Outputs:
- vectors: float32 [262144, 128], P(('grp', 'blk'))
Inputs may be any that keep to these rules, and one draw needn't show every extreme that they name: need_blocks[d, h] is -1 for d's own group and for groups d reads nothing from, else a row block index below 4 of the device of group h at d's position along blk; every device reads from at least one other group. far_groups[d, t] is a group h with need_blocks[d, h] >= 0.
All inputs are finite; a program needn't handle non-finite values.
Results may differ from a plain program's by a relative error of at most 0.0029.
Values may be sent and summed in bfloat16 or wider, within the bound.
A program may use at most 128 MiB of HBM per device.

v0:
```python
import jax
import jax.numpy as jnp
from jax import lax
from jax.sharding import PartitionSpec as P

ITERS = 2


def per_device(tiles_near, near_cols, tiles_far, far_groups, need_blocks, start_vectors):
    tile_size = tiles_near.shape[1]
    vec_width = start_vectors.shape[1]
    blocks = start_vectors.shape[0] // tile_size
    group_size = lax.axis_size("blk")
    group_count = lax.axis_size("grp")
    per_source = tiles_near.shape[0] // (blocks * group_size)
    far_each = tiles_far.shape[0] // blocks
    near_tiles = tiles_near.reshape(blocks, group_size, per_source, tile_size, tile_size)
    near_index = near_cols.reshape(blocks, group_size, per_source)
    far_tiles = tiles_far.reshape(blocks, far_each, tile_size, tile_size)
    far_index = far_groups.reshape(blocks, far_each)
    wanted = need_blocks.reshape(group_count)
    total_rows = blocks * tile_size * group_size * group_count
    current = start_vectors
    vectors = start_vectors.astype(jnp.float32)
    for iteration in range(ITERS):
        local_rows = current.reshape(blocks, tile_size, vec_width)
        group_table = lax.all_gather(local_rows, "blk", axis=0, tiled=True)
        source_ids = jnp.arange(group_size, dtype=jnp.int32)[None, :, None]
        chosen = group_table[source_ids * blocks + near_index]
        near_part = jnp.einsum(
            "rmnij,rmnjk->rik", near_tiles, chosen, preferred_element_type=jnp.float32
        )
        everything = lax.all_gather(local_rows, "grp", axis=0, tiled=True)
        far_rows = everything[far_index * blocks + wanted[far_index]]
        far_part = jnp.einsum(
            "rnij,rnjk->rik", far_tiles, far_rows, preferred_element_type=jnp.float32
        )
        product = near_part + far_part
        flat_rows = product.reshape(blocks * tile_size, vec_width)
        local_gram = jnp.dot(
            flat_rows.T,
            flat_rows,
            precision=lax.Precision.HIGHEST,
            preferred_element_type=jnp.float32,
        )
        gram = lax.psum(local_gram, ("grp", "blk")) / total_rows
        factor = jnp.linalg.cholesky(gram)
        identity_matrix = jnp.eye(vec_width, dtype=jnp.float32)
        inverse = lax.linalg.triangular_solve(factor, identity_matrix, left_side=True, lower=True).T
        vectors = jnp.dot(
            flat_rows, inverse, precision=lax.Precision.HIGHEST, preferred_element_type=jnp.float32
        )
        current = vectors.astype(jnp.bfloat16)
    return vectors


def solution(mesh):
    in_specs = (
        P(("grp", "blk"), None, None),
        P(("grp", "blk"), None),
        P(("grp", "blk"), None, None),
        P(("grp", "blk"), None),
        P(("grp", "blk"), None),
        P(("grp", "blk"), None),
    )
    out_specs = P(("grp", "blk"), None)
    return jax.shard_map(
        per_device, mesh=mesh, in_specs=in_specs, out_specs=out_specs, check_vma=False
    )
```

profile of v0, /device:TPU:1, one launch (start us, length us, event | category | flops | bytes accessed | tf_op | source)
XLA Modules:
  0.0 777.3 jit_solution(7489281376360508679)
XLA Ops:
  6.5 0.0 copy-start
  6.5 0.7 all-gather.5.cloned.1.call-update
  7.3 0.0 all-gather.7.cloned.1.call-start
  7.3 0.7 all-gather.7.cloned.1.call-update
  8.0 0.0 all-reduce.3.cloned.1.call-start
  8.1 0.5 broadcast.166
  8.6 1.3 reduce.10
  9.9 0.1 reshape.119
  10.0 0.1 reshape.137
  10.1 1.4 gather_fusion.1
  11.4 0.1 gather.20
  11.5 0.1 reshape.145
  11.6 1.3 reduce.11
  12.9 0.1 reshape.117
  13.1 0.1 compare_select_fusion
  13.1 0.1 reshape.129
  13.3 37.1 %all-gather.5.cloned.1.call-done = bf16[32,256,128]{2,1,0:T(8,128)(2,1)} async-done(((bf16[4,256,128]{2,1,0:T(8,128)(2,1)}), bf16[32,256,128]{2,1,0:T(8,128)(2,1)}) %all-gather.5.cloned.1.call-update) | async-done | bytes 2097168 | tf_op jit(solution)/shard_map/all_gather | solution.py:27
  50.4 4.6 gather_fusion
  55.0 58.5 %all-gather.7.cloned.1.call-done = bf16[128,256,128]{2,1,0:T(8,128)(2,1)} async-done(((bf16[4,256,128]{2,1,0:T(8,128)(2,1)}), bf16[128,256,128]{2,1,0:T(8,128)(2,1)}) %all-gather.7.cloned.1.call-update) | async-done | bytes 8388624 | tf_op jit(solution)/shard_map/all_gather | solution.py:33
  113.6 5.4 gather_fusion.2
  118.9 2.7 convolution_bitcast_fusion.1
  121.7 0.0 copy-done.4
  121.7 5.2 fusion.31
  126.9 0.0 copy-start.1
  126.9 0.8 copy-done.1
  127.7 1.2 convolution_bitcast_fusion.3
  128.9 0.0 all-reduce.3.cloned.1.call-update
  128.9 0.0 all-gather.9.cloned.1.call-start
  129.0 2.0 copy.32
  131.0 235.3 %all-reduce.3.cloned.1.call-done = f32[128,128]{0,1:T(8,128)} async-done(((f32[128,128]{0,1:T(8,128)}), f32[128,128]{0,1:T(8,128)}) %all-reduce.3.cloned.1.call-update) | async-done | bytes 65552 | tf_op jit(solution)/shard_map/psum | solution.py:46
  366.3 0.8 broadcast_multiply_fusion.1
  367.2 0.1 copy.35
  367.3 0.9 fusion.45
  368.1 11.7 %cholesky.44 = f32[128,128]{1,0:T(8,128)S(1)} custom-call(f32[128,128]{1,0:T(8,128)S(1)} %fusion.45), custom_call_target="Cholesky" | custom-call | tf_op jit(solution)/shard_map/jit(cholesky)/cholesky | solution.py:47
  379.9 0.6 compare_reduce_fusion.1
  380.5 0.7 fusion.40
  381.2 9.8 %custom-call.6 = f32[1,128,128]{1,2,0:T(8,128)S(1)} custom-call(f32[1,128,128]{2,1,0:T(8,128)S(1)} %fusion.40), custom_call_target="InvertDiagBlocksLowerTriangular" | custom-call | tf_op jit(solution)/shard_map/triangular_solve/custom-call.0 | solution.py:49
  391.0 0.3 fusion.38
  391.3 2.3 convolution_convert_fusion
  393.6 0.0 all-gather.9.cloned.1.call-update
  393.6 0.0 all-gather.11.cloned.1.call-start
  393.7 0.5 all-gather.11.cloned.1.call-update
  394.2 0.2 all-reduce.5.cloned.1.call-start
  394.5 32.8 %all-gather.9.cloned.1.call-done = bf16[32,256,128]{2,1,0:T(8,128)(2,1)} async-done(((bf16[4,256,128]{2,1,0:T(8,128)(2,1)}), bf16[32,256,128]{2,1,0:T(8,128)(2,1)}) %all-gather.9.cloned.1.call-update) | async-done | bytes 2097168 | tf_op jit(solution)/shard_map/all_gather | solution.py:27
  427.3 4.6 gather_fusion.3
  432.0 58.4 %all-gather.11.cloned.1.call-done = bf16[128,256,128]{2,1,0:T(8,128)(2,1)} async-done(((bf16[4,256,128]{2,1,0:T(8,128)(2,1)}), bf16[128,256,128]{2,1,0:T(8,128)(2,1)}) %all-gather.11.cloned.1.call-update) | async-done | bytes 8388624 | tf_op jit(solution)/shard_map/all_gather | solution.py:33
  490.3 5.4 gather_fusion.4
  495.7 2.7 convolution_bitcast_fusion
  498.4 5.2 fusion.21
  503.7 0.0 copy-start.2
  503.7 0.8 copy-done.2
  504.5 1.2 convolution_bitcast_fusion.2
  505.7 0.0 all-reduce.5.cloned.1.call-update
  505.7 2.0 copy.39
  507.7 235.3 %all-reduce.5.cloned.1.call-done = f32[128,128]{0,1:T(8,128)} async-done(((f32[128,128]{0,1:T(8,128)}), f32[128,128]{0,1:T(8,128)}) %all-reduce.5.cloned.1.call-update) | async-done | bytes 65552 | tf_op jit(solution)/shard_map/psum | solution.py:46
  743.1 0.8 broadcast_multiply_fusion
  743.9 0.1 copy.42
  744.0 0.9 fusion.43
  744.9 11.7 %cholesky.55 = f32[128,128]{1,0:T(8,128)S(1)} custom-call(f32[128,128]{1,0:T(8,128)S(1)} %fusion.43), custom_call_target="Cholesky" | custom-call | tf_op jit(solution)/shard_map/jit(cholesky)/cholesky | solution.py:47
  756.6 0.6 compare_reduce_fusion
  757.2 0.7 fusion.41
  757.9 9.8 %custom-call.7 = f32[1,128,128]{1,2,0:T(8,128)S(1)} custom-call(f32[1,128,128]{2,1,0:T(8,128)S(1)} %fusion.41), custom_call_target="InvertDiagBlocksLowerTriangular" | custom-call | tf_op jit(solution)/shard_map/triangular_solve/custom-call.0 | solution.py:49
  767.7 0.3 fusion.36
  768.0 2.4 fusion.46
  (13 shorter events, 0.1 us)
Async XLA Ops:
  6.5 112.4 %copy-start = (bf16[24,256,256]{2,1,0:T(8,128)(2,1)S(1)}, bf16[24,256,256]{2,1,0:T(8,128)(2,1)}, u32[]{:S(2)}) copy-start(bf16[24,256,256]{2,1,0:T(8,128)(2,1)} %param.11) | copy-start | bytes 9437188
  6.5 43.8 %all-gather.5.cloned.1.call-start = ((), (), s32[]{:S(2)}) async-start(), calls=%async_computation | async-start | bytes 2359296 | tf_op jit(solution)/shard_map/all_gather | solution.py:27
  7.3 106.3 %all-gather.7.cloned.1.call-start = ((), (), s32[]{:S(2)}) async-start(), calls=%async_computation.1 | async-start | bytes 8650752 | tf_op jit(solution)/shard_map/all_gather | solution.py:33
  8.0 358.3 %all-reduce.3.cloned.1.call-start = ((), (), s32[]{:S(2)}) async-start(), calls=%async_computation.2 | async-start | bytes 131072 | tf_op jit(solution)/shard_map/psum | solution.py:46
  118.9 2.7 copy-start.4
  126.9 0.8 copy-start.1
  128.9 298.4 %all-gather.9.cloned.1.call-start = ((), (), s32[]{:S(2)}) async-start(), calls=%async_computation.3 | async-start | bytes 2359296 | tf_op jit(solution)/shard_map/all_gather | solution.py:27
  393.6 96.7 %all-gather.11.cloned.1.call-start = ((), (), s32[]{:S(2)}) async-start(), calls=%async_computation.4 | async-start | bytes 8650752 | tf_op jit(solution)/shard_map/all_gather | solution.py:33
  394.2 348.8 %all-reduce.5.cloned.1.call-start = ((), (), s32[]{:S(2)}) async-start(), calls=%async_computation.5 | async-start | bytes 131072 | tf_op jit(solution)/shard_map/psum | solution.py:46
  495.7 2.7 copy-start.3
  503.7 0.8 copy-start.2
Sparse Core Ops, SparseCore 0:
  9.1 41.1 all-gather.4
  52.9 60.5 all-gather.6
  129.1 237.2 all-reduce.2
  393.8 33.4 all-gather.8
  429.7 60.5 all-gather.10
  505.8 237.1 all-reduce.4
where the time goes:
time: 778 us; the launch traced here: 777 us
  waiting for transfers between devices  659 us (85%)
  other arithmetic  51.9 us (7%)
  local copies, waits for them, and re-layouts  28.3 us (4%)
  matrix products  23.6 us (3%)
  between operations  13.7 us (2%)
    psum x2, waiting for transfers between devices, per_device(): gram = lax.psum(local_gram, ('grp', 'blk')) / total_rows  471 us
    all_gather x2, waiting for transfers between devices, per_device(): everything = lax.all_gather(local_rows, 'grp', axis=0, tiled=True)  117 us
    all_gather x2, waiting for transfers between devices, per_device(): group_table = lax.all_gather(local_rows, 'blk', axis=0, tiled=True)  70 us
    another operation x6, other arithmetic, per_device(): factor = jnp.linalg.cholesky(gram)  24.8 us
    another operation x4, other arithmetic, per_device(): lax.linalg.triangular_solve(factor, identity_matrix, left_side=True, lowe...  20.9 us
  transfers between devices with their start and end apart: 6, of which 6 were waited for; matrix products, arithmetic and copies ran while one was open for 2% of the time, Pallas kernels for 0%

commit v1 on v0

--- a/solution.py
+++ b/solution.py
@@ -43,7 +43,7 @@
             precision=lax.Precision.HIGHEST,
             preferred_element_type=jnp.float32,
         )
-        gram = lax.psum(local_gram, ("grp", "blk")) / total_rows
+        gram = jnp.sum(lax.all_gather(local_gram, ("grp", "blk")), axis=0) / total_rows
         factor = jnp.linalg.cholesky(gram)
         identity_matrix = jnp.eye(vec_width, dtype=jnp.float32)
         inverse = lax.linalg.triangular_solve(factor, identity_matrix, left_side=True, lower=True).T

time: 778 us -> 563 us (0.72)
  waiting for transfers between devices: 659 us -> 435 us
  other arithmetic: 51.9 us -> 61.7 us
    psum x2 -> x0, waiting for transfers between devices: 471 us -> none  [per_device(): gram = lax.psum(local_gram, ('grp', 'blk')) / total_rows]
    all_gather x0 -> x2, waiting for transfers between devices: none -> 245 us  [per_device(): lax.all_gather(local_gram, ('grp', 'blk'))]
    reduce_sum x0 -> x2, other arithmetic: none -> 13.2 us  [per_device(): jnp.sum(lax.all_gather(local_gram, ('grp', 'blk')), axis=0) / total_rows]
  transfers between devices with their start and end apart: 6 -> 6, of which waited for: 6 -> 6; matrix products, arithmetic and copies ran while one was open for 2% -> 3% of each run, Pallas kernels for 0% -> 0%
where the time goes in v1:
time: 563 us
  waiting for transfers between devices  435 us (77%)
  other arithmetic  61.7 us (11%)
  local copies, waits for them, and re-layouts  28.5 us (5%)
  matrix products  23.6 us (4%)
  between operations  13.7 us (2%)
    all_gather x2, waiting for transfers between devices, per_device(): lax.all_gather(local_gram, ('grp', 'blk'))  245 us
    all_gather x2, waiting for transfers between devices, per_device(): everything = lax.all_gather(local_rows, 'grp', axis=0, tiled=True)  117 us
    all_gather x2, waiting for transfers between devices, per_device(): group_table = lax.all_gather(local_rows, 'blk', axis=0, tiled=True)  70.7 us
    another operation x6, other arithmetic, per_device(): factor = jnp.linalg.cholesky(gram)  24.8 us
    another operation x4, other arithmetic, per_device(): lax.linalg.triangular_solve(factor, identity_matrix, left_side=True, lowe...  20.9 us
    reduce_sum x2, other arithmetic, per_device(): jnp.sum(lax.all_gather(local_gram, ('grp', 'blk')), axis=0) / total_rows  13.2 us
    gather x4, local copies, waits for them, and re-layouts, per_device(): far_rows = everything[far_index * blocks + wanted[far_index]]  12.2 us
  transfers between devices with their start and end apart: 6, of which 6 were waited for; matrix products, arithmetic and copies ran while one was open for 3% of the time, Pallas kernels for 0%

profile of v1, /device:TPU:1, one launch (start us, length us, event | category | flops | bytes accessed | tf_op | source)
XLA Modules:
  0.0 562.6 jit_solution(3628210382297687145)
XLA Ops:
  6.5 0.7 all-gather.9.cloned.1.call-update
  7.3 0.0 all-gather.11.cloned.1.call-start
  7.3 0.7 all-gather.11.cloned.1.call-update
  8.0 0.0 all-gather.17.cloned.1.call-start
  8.1 0.5 broadcast.166
  8.6 1.3 reduce.11
  9.9 1.3 reduce.10
  11.2 0.1 reshape.119
  11.3 0.1 reshape.137
  11.4 1.4 gather_fusion.1
  12.7 0.1 gather.20
  12.8 0.1 reshape.145
  12.9 0.1 reshape.117
  13.1 0.1 compare_select_fusion
  13.1 0.1 reshape.129
  13.3 37.1 %all-gather.9.cloned.1.call-done = bf16[32,256,128]{2,1,0:T(8,128)(2,1)} async-done(((bf16[4,256,128]{2,1,0:T(8,128)(2,1)}), bf16[32,256,128]{2,1,0:T(8,128)(2,1)}) %all-gather.9.cloned.1.call-update) | async-done | bytes 2097168 | tf_op jit(solution)/shard_map/all_gather | solution.py:27
  50.4 4.6 gather_fusion
  55.0 58.5 %all-gather.11.cloned.1.call-done = bf16[128,256,128]{2,1,0:T(8,128)(2,1)} async-done(((bf16[4,256,128]{2,1,0:T(8,128)(2,1)}), bf16[128,256,128]{2,1,0:T(8,128)(2,1)}) %all-gather.11.cloned.1.call-update) | async-done | bytes 8388624 | tf_op jit(solution)/shard_map/all_gather | solution.py:33
  113.6 5.4 gather_fusion.2
  118.9 2.7 convolution_bitcast_fusion.1
  121.7 0.0 copy-done.4
  121.7 5.2 fusion.31
  126.9 0.0 copy-start.1
  126.9 0.8 copy-done.1
  127.7 1.2 convolution_bitcast_fusion.3
  128.9 0.0 all-gather.17.cloned.1.call-update
  128.9 0.0 all-gather.13.cloned.1.call-start
  129.0 2.0 copy.28
  131.0 122.5 %all-gather.17.cloned.1.call-done = f32[32768,128]{1,0:T(8,128)} async-done(((f32[128,128]{1,0:T(8,128)}), f32[32768,128]{1,0:T(8,128)}) %all-gather.17.cloned.1.call-update) | async-done | bytes 16777232 | tf_op jit(solution)/shard_map/all_gather | solution.py:46
  253.6 6.6 %reduce_sum.18 = f32[128,128]{1,0:T(8,128)S(1)} reduce(f32[256,128,128]{2,1,0:T(8,128)} %bitcast.84, f32[]{:T(128)} %constant.44.clone.1), dimensions={0}, to_apply=%region_0.0 | reduce | flops 4177920 | bytes 16842756 | tf_op jit(solution)/shard_map/reduce_sum | solution.py:46
  260.2 0.1 copy.30
  260.3 0.1 copy.31
  260.4 11.7 %cholesky.44 = f32[128,128]{1,0:T(8,128)S(1)} custom-call(f32[128,128]{1,0:T(8,128)S(1)} %fusion.45), custom_call_target="Cholesky" | custom-call | tf_op jit(solution)/shard_map/jit(cholesky)/cholesky | solution.py:47
  272.1 0.6 compare_reduce_fusion.1
  272.8 0.7 fusion.40
  273.4 9.8 %custom-call.6 = f32[1,128,128]{1,2,0:T(8,128)S(1)} custom-call(f32[1,128,128]{2,1,0:T(8,128)S(1)} %fusion.40), custom_call_target="InvertDiagBlocksLowerTriangular" | custom-call | tf_op jit(solution)/shard_map/triangular_solve/custom-call.0 | solution.py:49
  283.3 0.3 fusion.38
  283.5 2.3 convolution_convert_fusion
  285.9 0.0 all-gather.13.cloned.1.call-update
  285.9 0.0 all-gather.15.cloned.1.call-start
  286.0 0.5 all-gather.15.cloned.1.call-update
  286.5 0.2 all-gather.19.cloned.1.call-start
  286.7 33.6 %all-gather.13.cloned.1.call-done = bf16[32,256,128]{2,1,0:T(8,128)(2,1)} async-done(((bf16[4,256,128]{2,1,0:T(8,128)(2,1)}), bf16[32,256,128]{2,1,0:T(8,128)(2,1)}) %all-gather.13.cloned.1.call-update) | async-done | bytes 2097168 | tf_op jit(solution)/shard_map/all_gather | solution.py:27
  320.3 4.6 gather_fusion.3
  325.0 58.4 %all-gather.15.cloned.1.call-done = bf16[128,256,128]{2,1,0:T(8,128)(2,1)} async-done(((bf16[4,256,128]{2,1,0:T(8,128)(2,1)}), bf16[128,256,128]{2,1,0:T(8,128)(2,1)}) %all-gather.15.cloned.1.call-update) | async-done | bytes 8388624 | tf_op jit(solution)/shard_map/all_gather | solution.py:33
  383.3 5.4 gather_fusion.4
  388.7 2.7 convolution_bitcast_fusion
  391.5 0.0 copy-done.3
  391.5 5.2 fusion.21
  396.7 0.0 copy-start.2
  396.7 0.8 copy-done.2
  397.5 1.2 convolution_bitcast_fusion.2
  398.7 0.0 all-gather.19.cloned.1.call-update
  398.7 2.0 copy.35
  400.8 122.6 %all-gather.19.cloned.1.call-done = f32[32768,128]{1,0:T(8,128)} async-done(((f32[128,128]{1,0:T(8,128)}), f32[32768,128]{1,0:T(8,128)}) %all-gather.19.cloned.1.call-update) | async-done | bytes 16777232 | tf_op jit(solution)/shard_map/all_gather | solution.py:46
  523.4 6.6 %reduce_sum.19 = f32[128,128]{1,0:T(8,128)S(1)} reduce(f32[256,128,128]{2,1,0:T(8,128)} %bitcast.85, f32[]{:T(128)} %constant.44.clone.1), dimensions={0}, to_apply=%region_3.6 | reduce | flops 4177920 | bytes 16842756 | tf_op jit(solution)/shard_map/reduce_sum | solution.py:46
  529.9 0.1 copy.37
  530.1 0.1 copy.38
  530.2 11.7 %cholesky.55 = f32[128,128]{1,0:T(8,128)S(1)} custom-call(f32[128,128]{1,0:T(8,128)S(1)} %fusion.43), custom_call_target="Cholesky" | custom-call | tf_op jit(solution)/shard_map/jit(cholesky)/cholesky | solution.py:47
  541.9 0.6 compare_reduce_fusion
  542.6 0.7 fusion.41
  543.2 9.8 %custom-call.7 = f32[1,128,128]{1,2,0:T(8,128)S(1)} custom-call(f32[1,128,128]{2,1,0:T(8,128)S(1)} %fusion.41), custom_call_target="InvertDiagBlocksLowerTriangular" | custom-call | tf_op jit(solution)/shard_map/triangular_solve/custom-call.0 | solution.py:49
  553.0 0.3 fusion.36
  553.3 2.4 fusion.46
  (17 shorter events, 0.2 us)
Async XLA Ops:
  6.5 112.4 %copy-start = (bf16[24,256,256]{2,1,0:T(8,128)(2,1)S(1)}, bf16[24,256,256]{2,1,0:T(8,128)(2,1)}, u32[]{:S(2)}) copy-start(bf16[24,256,256]{2,1,0:T(8,128)(2,1)} %param.11) | copy-start | bytes 9437188
  6.5 43.8 %all-gather.9.cloned.1.call-start = ((), (), s32[]{:S(2)}) async-start(), calls=%async_computation | async-start | bytes 2359296 | tf_op jit(solution)/shard_map/all_gather | solution.py:27
  7.3 106.3 %all-gather.11.cloned.1.call-start = ((), (), s32[]{:S(2)}) async-start(), calls=%async_computation.1 | async-start | bytes 8650752 | tf_op jit(solution)/shard_map/all_gather | solution.py:33
  8.0 245.6 %all-gather.17.cloned.1.call-start = ((), (), s32[]{:S(2)}) async-start(), calls=%async_computation.4 | async-start | bytes 16842752 | tf_op jit(solution)/shard_map/all_gather | solution.py:46
  118.9 2.7 copy-start.4
  126.9 0.8 copy-start.1
  128.9 191.4 %all-gather.13.cloned.1.call-start = ((), (), s32[]{:S(2)}) async-start(), calls=%async_computation.2 | async-start | bytes 2359296 | tf_op jit(solution)/shard_map/all_gather | solution.py:27
  285.9 97.4 %all-gather.15.cloned.1.call-start = ((), (), s32[]{:S(2)}) async-start(), calls=%async_computation.3 | async-start | bytes 8650752 | tf_op jit(solution)/shard_map/all_gather | solution.py:33
  286.5 236.9 %all-gather.19.cloned.1.call-start = ((), (), s32[]{:S(2)}) async-start(), calls=%async_computation.5 | async-start | bytes 16842752 | tf_op jit(solution)/shard_map/all_gather | solution.py:46
  388.7 2.7 copy-start.3
  396.7 0.8 copy-start.2
Sparse Core Ops, SparseCore 0:
  9.1 41.1 all-gather.8
  52.9 60.5 all-gather.10
  129.1 124.4 all-gather.16
  286.0 34.2 all-gather.12
  322.7 60.5 all-gather.14
  398.8 124.4 all-gather.18
